TPU v7x, 512 devices: a whole 4x4x16 slice. The times are simulated.
512 devices in a mesh: section: 16 (over z), row: 8 (over y, core), col: 4 (over x).
Axes of the slice: x: 4, y: 4, z: 16, core: 2. Of those that a mesh axis runs over, the one named last changes fastest.
Arguments:
- x_fwd: bfloat16 [4096, 12288], P('section', 'row'), may hold values from -6 to 6
- dy_bwd: bfloat16 [4096, 12288], P(('section', 'row'), 'col'), may hold values from -6 to 6
- w_blocks: bfloat16 [16, 8, 4, 115, 128, 128], P('section', 'row', 'col'), may hold values from -0.09375 to 0.09375
- blk_row: int32 [16, 8, 4, 115], P('section', 'row', 'col'), may hold values from 0 to 11, as said below
- blk_col: int32 [16, 8, 4, 115], P('section', 'row', 'col'), may hold values from 0 to 23, as said below
- blk_count: int32 [16, 8, 4], P('section', 'row', 'col'), may hold values from 57 to 115, as said below
- tok_count: int32 [16, 2], P('section'), may hold values from 64 to 256, as said below
- owner_order: int32 [16, 64], P('section'), may hold values from 0 to 63, each once within a row
Outputs:
- y_next: bfloat16 [4096, 12288], P(('section', 'row', 'col'))
- dx_section: bfloat16 [4096, 12288], P(('section', 'row', 'col'))
Inputs may be any that keep to these rules, and one draw needn't show every extreme that they name: At each grid position the slots below blk_count name distinct block positions (blk_row, blk_col); the other slots name arbitrary positions. `blk_col`: see blk_row. `blk_count`: some grid position of every draw holds exactly 115 live slots. `tok_count`: index 0 counts the forward micro-batch, index 1 the backward one; valid tokens come first; some entry of every draw equals 256. `owner_order`: each section's row is a permutation.
All inputs are finite; a program needn't handle non-finite values.
Results may differ from a plain program's by a relative error of at most 0.015.
Values may be sent and summed in bfloat16 or wider, within the bound.
A program may use at most 128 MiB of HBM per device.

v0:
```python
import jax
import jax.numpy as jnp
from jax import lax
from jax.sharding import PartitionSpec as P


def passed_along(shard, axis, by):
    length = lax.axis_size(axis)
    pairs = [(i, i + by) for i in range(length) if 0 <= i + by < length]
    return lax.ppermute(shard, axis, pairs)


def local(x_fwd, dy_bwd, w_blocks, blk_row, blk_col, blk_count, tok_count, owner_order):
    row_count = lax.axis_size("row")
    col_count = lax.axis_size("col")
    token_total, in_width = x_fwd.shape
    out_width = dy_bwd.shape[1]
    slot_total = w_blocks.shape[3]
    block_size = w_blocks.shape[5]
    block_rows = in_width // block_size
    block_cols = out_width // block_size
    owned_rows = token_total // (row_count * col_count)
    weights = w_blocks.reshape(slot_total, block_size, block_size)
    live = (jnp.arange(slot_total) < blk_count.reshape(())).astype(weights.dtype)
    dense_blocks = jnp.zeros((block_rows, block_cols, block_size, block_size), weights.dtype)
    dense_blocks = dense_blocks.at[blk_row.reshape(slot_total), blk_col.reshape(slot_total)].add(
        weights * live[:, None, None]
    )
    dense_weight = jnp.transpose(dense_blocks, (0, 2, 1, 3)).reshape(in_width, out_width)
    limits = tok_count.reshape(2)
    block_total = owner_order.shape[1]
    block_length = token_total // block_total
    token_index = (
        owner_order.reshape(block_total)[:, None] * block_length + jnp.arange(block_length)[None, :]
    ).reshape(token_total)
    ordered_rows = jnp.take(x_fwd, token_index, axis=0)
    ordered_rows = jnp.where(
        (token_index < limits[0])[:, None], ordered_rows, jnp.zeros_like(ordered_rows)
    )
    partial_value = jnp.dot(ordered_rows, dense_weight, preferred_element_type=jnp.float32).astype(
        jnp.bfloat16
    )
    outgoing = partial_value.reshape(row_count * col_count, owned_rows, out_width)
    received = lax.all_to_all(outgoing, ("row", "col"), split_axis=0, concat_axis=2, tiled=True)
    summed = received.reshape(owned_rows, row_count, col_count * out_width).astype(jnp.float32)
    forward_act = jnp.sum(summed, axis=1).astype(jnp.bfloat16)
    y_next = passed_along(forward_act, "section", 1)
    grad_rows = dy_bwd.shape[0]
    grad_index = lax.axis_index("row") * grad_rows + jnp.arange(grad_rows)
    grad_kept = jnp.where((grad_index < limits[1])[:, None], dy_bwd, jnp.zeros_like(dy_bwd))
    grad_partial = lax.dot_general(
        lax.all_gather(grad_kept, "row", axis=0, tiled=True),
        dense_weight,
        (((1,), (1,)), ((), ())),
        preferred_element_type=jnp.float32,
    ).astype(jnp.bfloat16)
    grad_outgoing = grad_partial.reshape(row_count * col_count, owned_rows, in_width)
    grad_received = lax.all_to_all(
        grad_outgoing, ("row", "col"), split_axis=0, concat_axis=2, tiled=True
    )
    grad_summed = grad_received.reshape(owned_rows, row_count, col_count, in_width).astype(
        jnp.float32
    )
    dx_section = (
        jnp.sum(grad_summed, axis=2).reshape(owned_rows, row_count * in_width).astype(jnp.bfloat16)
    )
    return (y_next, dx_section)


def solution(mesh):
    return jax.shard_map(
        local,
        mesh=mesh,
        in_specs=(
            P("section", "row"),
            P(("section", "row"), "col"),
            P("section", "row", "col", None, None, None),
            P("section", "row", "col", None),
            P("section", "row", "col", None),
            P("section", "row", "col"),
            P("section", None),
            P("section", None),
        ),
        out_specs=(P(("section", "row", "col"), None), P(("section", "row", "col"), None)),
        check_vma=False,
    )
```

profile of v0, /device:TPU:1, one launch (start us, length us, event | category | flops | bytes accessed | tf_op | source)
XLA Modules:
  0.0 134.2 jit_solution(12094650554060465217)
XLA Ops:
  7.2 0.0 copy-start
  7.2 0.0 all-gather.2.cloned.1.call-start
  7.2 1.3 fusion.28
  8.5 0.7 add_compare_fusion
  9.2 1.7 %broadcast_select_fusion = bf16[32,3072]{1,0:T(8,128)(2,1)} fusion(bf16[32,3072]{1,0:T(8,128)(2,1)} %param.9, pred[32]{0:T(512)(128)(4,1)S(1)} %add_compare_fusion), kind=kLoop, calls=%fused_computation.20 | loop fusion | flops 98304 | bytes 393248 | tf_op jit(solution)/shard_map/jit(_where)/select_n | solution.py:50
  10.9 0.0 all-gather.2.cloned.1.call-update
  11.6 0.7 multiply_bitcast_fusion
  12.2 0.1 iota_add_fusion
  12.3 0.1 add.97
  12.4 0.1 add.94
  12.5 0.7 fusion.25
  13.2 4.2 %bitcast_multiply_fusion = bf16[115,128,128]{2,1,0:T(8,128)(2,1)} fusion(bf16[1,1,1,115,128,128]{5,4,3,2,1,0:T(8,128)(2,1)} %param.10, bf16[115]{0:T(256)(128)(2,1)S(1)} %compare_convert_fusion), kind=kLoop, calls=%fused_computation.9 | loop fusion | flops 1884160 | bytes 7536870 | tf_op jit(solution)/shard_map/mul | solution.py:27
  17.4 6.0 %broadcast_in_dim.45 = bf16[12,24,128,128]{3,2,1,0:T(8,128)(2,1)} broadcast(bf16[]{:T(256)} %constant.9.clone.1), dimensions={} | broadcast | bytes 9437186 | tf_op jit(solution)/shard_map/broadcast_in_dim | solution.py:25
  23.4 27.2 %scatter_fusion = bf16[12,24,128,128]{3,2,1,0:T(8,128)(2,1)} fusion(bf16[12,24,128,128]{3,2,1,0:T(8,128)(2,1)} %broadcast_in_dim.45, s32[115]{0:T(128)S(1)} %fusion.25, bf16[115,128,128]{2,1,0:T(8,128)(2,1)} %bitcast_multiply_fusion), kind=kCustom, calls=%fused_computation.1 | custom fusion | flops 1884160 | bytes 11305880 | tf_op jit(solution)/shard_map/scatter-add | solution.py:26
  50.6 14.6 %copy.13 = bf16[12,128,24,128]{3,2,1,0:T(8,128)(2,1)} copy(bf16[12,128,24,128]{3,1,2,0:T(8,128)(2,1)} %bitcast.52) | data formatting | bytes 18874368 | tf_op jit(solution)/shard_map/transpose | solution.py:29
  65.2 0.0 copy-done
  65.3 1.3 gather_fusion
  66.5 0.6 broadcast_compare_fusion
  67.2 7.5 %fusion.9 = bf16[32,8,3072]{2,1,0:T(8,128)(2,1)} fusion(bf16[192,8,24,128]{3,2,1,0:T(8,128)(2,1)} %bitcast.53, bf16[256,1536]{1,0:T(8,128)(2,1)S(1)} %gather_fusion, pred[256]{0:T(512)(128)(4,1)S(1)} %get-tuple-element.3, pred[256]{0:T(512)(128)(4,1)S(1)} %get-tuple-element.2), kind=kOutput, calls=%fused_computation.10 | convolution fusion | flops 2417491968 | bytes 11796992 | tf_op jit(solution)/shard_map/dot_general | solution.py:40
  74.7 10.5 %all-to-all-start = ((bf16[32,8,3072]{2,1,0:T(8,128)(2,1)}), bf16[32,8,3072]{2,1,0:T(8,128)(2,1)S(1)}, u32[]{:S(2)}, u32[]{:S(2)}) async-start(bf16[32,8,3072]{2,1,0:T(8,128)(2,1)} %fusion.9), calls=%async_computation | async-start | bytes 3145728 | tf_op jit(solution)/shard_map/all_to_all | solution.py:44
  85.3 0.0 all-gather.2.cloned.1.call-done
  85.3 7.7 %fusion.15 = bf16[32,8,1536]{2,1,0:T(8,128)(2,1)} fusion(bf16[256,3072]{1,0:T(8,128)(2,1)} %all-gather.2.cloned.1.call-done, bf16[192,8,24,128]{3,2,1,0:T(8,128)(2,1)} %bitcast.54), kind=kOutput, calls=%fused_computation.12 | convolution fusion | flops 2416312320 | bytes 11796480 | tf_op jit(solution)/shard_map/dot_general | solution.py:51
  93.0 13.7 %all-to-all-done = bf16[32,8,3072]{2,1,0:T(8,128)(2,1)S(1)} async-done(((bf16[32,8,3072]{2,1,0:T(8,128)(2,1)}), bf16[32,8,3072]{2,1,0:T(8,128)(2,1)S(1)}, u32[]{:S(2)}, u32[]{:S(2)}) %all-to-all-start) | async-done | bytes 1572896 | tf_op jit(solution)/shard_map/all_to_all | solution.py:44
  106.7 5.6 %all-to-all-start.1 = ((bf16[32,8,1536]{2,1,0:T(8,128)(2,1)}), bf16[32,8,1536]{2,1,0:T(8,128)(2,1)S(1)}, u32[]{:S(2)}, u32[]{:S(2)}) async-start(bf16[32,8,1536]{2,1,0:T(8,128)(2,1)} %fusion.15), calls=%async_computation.1 | async-start | bytes 1572864 | tf_op jit(solution)/shard_map/all_to_all | solution.py:58
  112.3 2.0 %copy.14 = bf16[1,8,32,3072]{3,2,1,0:T(8,128)(2,1)} copy(bf16[1,8,32,3072]{3,1,2,0:T(8,128)(2,1)S(1)} %bitcast.55) | data formatting | bytes 3145728 | tf_op jit(solution)/shard_map/all_to_all | solution.py:44
  114.3 2.9 %reshape.169 = bf16[8,8,12288]{2,1,0:T(8,128)(2,1)S(1)} reshape(bf16[1,8,32,3072]{3,2,1,0:T(8,128)(2,1)} %copy.14) | data formatting | bytes 3145728 | tf_op jit(solution)/shard_map/reshape | solution.py:45
  117.2 1.0 reduce_sum.21
  118.3 1.5 %collective-permute-start = (bf16[8,12288]{1,0:T(8,128)(2,1)S(1)}, bf16[8,12288]{1,0:T(8,128)(2,1)S(1)}, u32[]{:S(2)}, u32[]{:S(2)}) collective-permute-start(bf16[8,12288]{1,0:T(8,128)(2,1)S(1)} %reduce_sum.21), channel_id=1, source_target_pairs={{0,32},{32,64},{64,96},{96,128},{128,160},{160,192},{192,224},{224... | collective-permute-start | bytes 589832 | tf_op jit(solution)/shard_map/ppermute | solution.py:10
  119.8 4.0 %collective-permute-done = bf16[8,12288]{1,0:T(8,128)(2,1)S(1)} collective-permute-done((bf16[8,12288]{1,0:T(8,128)(2,1)S(1)}, bf16[8,12288]{1,0:T(8,128)(2,1)S(1)}, u32[]{:S(2)}, u32[]{:S(2)}) %collective-permute-start) | collective-permute-done | bytes 196640 | tf_op jit(solution)/shard_map/ppermute | solution.py:10
  123.8 2.1 %all-to-all-done.1 = bf16[32,8,1536]{2,1,0:T(8,128)(2,1)S(1)} async-done(((bf16[32,8,1536]{2,1,0:T(8,128)(2,1)}), bf16[32,8,1536]{2,1,0:T(8,128)(2,1)S(1)}, u32[]{:S(2)}, u32[]{:S(2)}) %all-to-all-start.1) | async-done | bytes 786464 | tf_op jit(solution)/shard_map/all_to_all | solution.py:58
  125.9 0.8 bitcast_reduce_fusion
  126.7 0.7 copy.35
  (3 shorter events, 0.0 us)
Async XLA Ops:
  7.2 58.1 %copy-start = (bf16[256,1536]{1,0:T(8,128)(2,1)S(1)}, bf16[256,1536]{1,0:T(8,128)(2,1)}, u32[]{:S(2)}) copy-start(bf16[256,1536]{1,0:T(8,128)(2,1)} %param.8) | copy-start | bytes 2359300
  7.2 78.1 %all-gather.2.cloned.1.call-start = ((), (), s32[]{:S(2)}) async-start(), calls=%async_computation.2 | async-start | bytes 1769472 | tf_op jit(solution)/shard_map/all_gather | solution.py:52
  74.7 32.0 %all-to-all-start = ((bf16[32,8,3072]{2,1,0:T(8,128)(2,1)}), bf16[32,8,3072]{2,1,0:T(8,128)(2,1)S(1)}, u32[]{:S(2)}, u32[]{:S(2)}) async-start(bf16[32,8,3072]{2,1,0:T(8,128)(2,1)} %fusion.9), calls=%async_computation | async-start | bytes 3145728 | tf_op jit(solution)/shard_map/all_to_all | solution.py:44
  106.7 19.2 %all-to-all-start.1 = ((bf16[32,8,1536]{2,1,0:T(8,128)(2,1)}), bf16[32,8,1536]{2,1,0:T(8,128)(2,1)S(1)}, u32[]{:S(2)}, u32[]{:S(2)}) async-start(bf16[32,8,1536]{2,1,0:T(8,128)(2,1)} %fusion.15), calls=%async_computation.1 | async-start | bytes 1572864 | tf_op jit(solution)/shard_map/all_to_all | solution.py:58
  118.3 5.6 %collective-permute-start = (bf16[8,12288]{1,0:T(8,128)(2,1)S(1)}, bf16[8,12288]{1,0:T(8,128)(2,1)S(1)}, u32[]{:S(2)}, u32[]{:S(2)}) collective-permute-start(bf16[8,12288]{1,0:T(8,128)(2,1)S(1)} %reduce_sum.21), channel_id=1, source_target_pairs={{0,32},{32,64},{64,96},{96,128},{128,160},{160,192},{192,224},{224... | collective-permute-start | bytes 589832 | tf_op jit(solution)/shard_map/ppermute | solution.py:10
Sparse Core Ops, SparseCore 0:
  11.0 37.7 all-gather.1
where the time goes:
time: 135 us; the launch traced here: 134 us
  other arithmetic  37.6 us (28%)
  local copies, waits for them, and re-layouts  29.1 us (22%)
  waiting for transfers between devices  19.9 us (15%)
  starting transfers between devices  17.7 us (13%)
  matrix products  15.2 us (11%)
  between operations  14.8 us (11%)
    scatter-add x1, other arithmetic, local(): dense_blocks.at[blk_row.reshape(slot_total), blk_col.reshape(slot_total)]  27.2 us
    transpose x1, local copies, waits for them, and re-layouts, local(): jnp.transpose(dense_blocks, (0, 2, 1, 3)).reshape(in_width, out_width)  14.6 us
    all_to_all x1, waiting for transfers between devices, local(): lax.all_to_all(outgoing, ('row', 'col'), split_axis=0, concat_axis=2, til...  13.7 us
    all_to_all x1, starting transfers between devices, local(): lax.all_to_all(outgoing, ('row', 'col'), split_axis=0, concat_axis=2, til...  10.5 us
    dot_general x1, matrix products, local(): lax.dot_general(lax.all_gather(grad_kept, 'row', axis=0, tiled=True), den...  7.69 us
    dot_general x1, matrix products, local(): jnp.dot(ordered_rows, dense_weight, preferred_element_type=jnp.float32)  7.55 us
    broadcast_in_dim x1, local copies, waits for them, and re-layouts, local(): jnp.zeros((block_rows, block_cols, block_size, block_size), weights.dtype)  6.03 us
    all_to_all x1, starting transfers between devices, local(): lax.all_to_all(grad_outgoing, ('row', 'col'), split_axis=0, concat_axis=2...  5.56 us
  transfers between devices with their start and end apart: 4, of which 3 were waited for; matrix products, arithmetic and copies ran while one was open for 57% of the time, Pallas kernels for 0%

commit v1 on v0

--- a/solution.py
+++ b/solution.py
@@ -41,7 +41,15 @@
         jnp.bfloat16
     )
     outgoing = partial_value.reshape(row_count * col_count, owned_rows, out_width)
-    received = lax.all_to_all(outgoing, ("row", "col"), split_axis=0, concat_axis=2, tiled=True)
+    received = jnp.concatenate(
+        lax.all_to_all(
+            jnp.stack(jnp.split(outgoing, lax.axis_size(("row", "col")), axis=0)),
+            ("row", "col"),
+            0,
+            0,
+        ),
+        axis=2,
+    )
     summed = received.reshape(owned_rows, row_count, col_count * out_width).astype(jnp.float32)
     forward_act = jnp.sum(summed, axis=1).astype(jnp.bfloat16)
     y_next = passed_along(forward_act, "section", 1)

time: 135 us -> 154 us (1.14)
  local copies, waits for them, and re-layouts: 29.1 us -> 48.9 us
    unnamed x3 -> x34, local copies, waits for them, and re-layouts: 0.69 us -> 19.9 us
    another operation x0 -> x2, local copies, waits for them, and re-layouts: none -> 3.51 us  [the longest x1 2.89 us: local(): received.reshape(owned_rows, row_count, col_count * out_width)]
    all_to_all x1 -> x0, local copies, waits for them, and re-layouts: 2.04 us -> none  [local(): lax.all_to_all(outgoing, ('row', 'col'), split_axis=0, concat_axis=2, til...]
  transfers between devices with their start and end apart: 4 -> 4, of which waited for: 3 -> 3; matrix products, arithmetic and copies ran while one was open for 57% -> 62% of each run, Pallas kernels for 0% -> 0%
where the time goes in v1:
time: 154 us; the launch traced here: 153 us
  local copies, waits for them, and re-layouts  48.9 us (32%)
  other arithmetic  37.6 us (24%)
  waiting for transfers between devices  19.9 us (13%)
  starting transfers between devices  17.7 us (11%)
  between operations  14.8 us (10%)
  matrix products  14.1 us (9%)
    scatter-add x1, other arithmetic, local(): dense_blocks.at[blk_row.reshape(slot_total), blk_col.reshape(slot_total)]  27.2 us
    unnamed x34, local copies, waits for them, and re-layouts  19.9 us
    transpose x1, local copies, waits for them, and re-layouts, local(): jnp.transpose(dense_blocks, (0, 2, 1, 3)).reshape(in_width, out_width)  14.6 us
    all_to_all x1, waiting for transfers between devices, local(): lax.all_to_all(jnp.stack(jnp.split(outgoing, lax.axis_size(('row', 'col')...  13.7 us
    all_to_all x1, starting transfers between devices, local(): lax.all_to_all(jnp.stack(jnp.split(outgoing, lax.axis_size(('row', 'col')...  10.5 us
    dot_general x1, matrix products, local(): lax.dot_general(lax.all_gather(grad_kept, 'row', axis=0, tiled=True), den...  7.69 us
    dot_general x1, matrix products, local(): jnp.dot(ordered_rows, dense_weight, preferred_element_type=jnp.float32)  6.37 us
    broadcast_in_dim x1, local copies, waits for them, and re-layouts, local(): jnp.zeros((block_rows, block_cols, block_size, block_size), weights.dtype)  6.03 us
  transfers between devices with their start and end apart: 4, of which 3 were waited for; matrix products, arithmetic and copies ran while one was open for 62% of the time, Pallas kernels for 0%

profile of v1, /device:TPU:1, one launch (start us, length us, event | category | flops | bytes accessed | tf_op | source)
XLA Modules:
  0.0 152.9 jit_solution(10597015855336337134)
XLA Ops:
  7.2 0.0 copy-start
  7.2 0.0 all-gather.2.cloned.1.call-start
  7.2 1.3 fusion.25
  8.5 0.7 add_compare_fusion
  9.2 1.7 %broadcast_select_fusion = bf16[32,3072]{1,0:T(8,128)(2,1)} fusion(bf16[32,3072]{1,0:T(8,128)(2,1)} %param.9, pred[32]{0:T(512)(128)(4,1)S(1)} %add_compare_fusion), kind=kLoop, calls=%fused_computation.19 | loop fusion | flops 98304 | bytes 393248 | tf_op jit(solution)/shard_map/jit(_where)/select_n | solution.py:58
  10.9 0.0 all-gather.2.cloned.1.call-update
  10.9 0.7 multiply_bitcast_fusion
  11.6 0.1 iota_add_fusion
  11.7 0.1 add.97
  11.8 0.1 add.94
  12.5 0.7 fusion.22
  13.2 4.2 %bitcast_multiply_fusion = bf16[115,128,128]{2,1,0:T(8,128)(2,1)} fusion(bf16[1,1,1,115,128,128]{5,4,3,2,1,0:T(8,128)(2,1)} %param.10, bf16[115]{0:T(256)(128)(2,1)S(1)} %compare_convert_fusion), kind=kLoop, calls=%fused_computation.9 | loop fusion | flops 1884160 | bytes 7536870 | tf_op jit(solution)/shard_map/mul | solution.py:27
  17.4 6.0 %broadcast_in_dim.45 = bf16[12,24,128,128]{3,2,1,0:T(8,128)(2,1)} broadcast(bf16[]{:T(256)} %constant.9.clone.1), dimensions={} | broadcast | bytes 9437186 | tf_op jit(solution)/shard_map/broadcast_in_dim | solution.py:25
  23.5 27.2 %scatter_fusion = bf16[12,24,128,128]{3,2,1,0:T(8,128)(2,1)} fusion(bf16[12,24,128,128]{3,2,1,0:T(8,128)(2,1)} %broadcast_in_dim.45, s32[115]{0:T(128)S(1)} %fusion.22, bf16[115,128,128]{2,1,0:T(8,128)(2,1)} %bitcast_multiply_fusion), kind=kCustom, calls=%fused_computation.1 | custom fusion | flops 1884160 | bytes 11305880 | tf_op jit(solution)/shard_map/scatter-add | solution.py:26
  50.6 14.6 %copy.11 = bf16[12,128,24,128]{3,2,1,0:T(8,128)(2,1)} copy(bf16[12,128,24,128]{3,1,2,0:T(8,128)(2,1)} %bitcast.174) | data formatting | bytes 18874368 | tf_op jit(solution)/shard_map/transpose | solution.py:29
  65.3 0.0 copy-done
  65.3 1.3 gather_fusion
  66.5 0.6 broadcast_compare_fusion
  67.2 6.4 %fusion.6 = bf16[256,3072]{1,0:T(8,128)(2,1)S(1)} fusion(bf16[192,8,24,128]{3,2,1,0:T(8,128)(2,1)} %bitcast.175, bf16[256,1536]{1,0:T(8,128)(2,1)S(1)} %gather_fusion, pred[256]{0:T(512)(128)(4,1)S(1)} %get-tuple-element.3, pred[256]{0:T(512)(128)(4,1)S(1)} %get-tuple-element.2), kind=kOutput, calls=%fused_computation.8 | convolution fusion | flops 2417491968 | bytes 11796992 | tf_op jit(solution)/shard_map/dot_general | solution.py:40
  73.6 0.6 constant_dynamic-update-slice_fusion.31
  74.2 0.6 constant_dynamic-update-slice_fusion.30
  74.8 0.6 constant_dynamic-update-slice_fusion.29
  75.4 0.6 constant_dynamic-update-slice_fusion.28
  76.0 0.6 constant_dynamic-update-slice_fusion.27
  76.6 0.6 constant_dynamic-update-slice_fusion.26
  77.3 0.6 constant_dynamic-update-slice_fusion.25
  77.9 0.6 constant_dynamic-update-slice_fusion.24
  78.5 0.6 constant_dynamic-update-slice_fusion.23
  79.1 0.6 constant_dynamic-update-slice_fusion.22
  79.7 0.6 constant_dynamic-update-slice_fusion.21
  80.4 0.6 constant_dynamic-update-slice_fusion.20
  81.0 0.6 constant_dynamic-update-slice_fusion.19
  81.6 0.6 constant_dynamic-update-slice_fusion.18
  82.2 0.6 constant_dynamic-update-slice_fusion.17
  82.8 0.6 constant_dynamic-update-slice_fusion.16
  83.5 0.6 constant_dynamic-update-slice_fusion.15
  84.1 0.6 constant_dynamic-update-slice_fusion.14
  84.7 0.6 constant_dynamic-update-slice_fusion.13
  85.3 0.6 constant_dynamic-update-slice_fusion.12
  85.9 0.6 constant_dynamic-update-slice_fusion.11
  86.6 0.6 constant_dynamic-update-slice_fusion.10
  87.2 0.6 constant_dynamic-update-slice_fusion.9
  87.8 0.6 constant_dynamic-update-slice_fusion.8
  88.4 0.6 constant_dynamic-update-slice_fusion.7
  89.0 0.6 constant_dynamic-update-slice_fusion.6
  89.7 0.6 constant_dynamic-update-slice_fusion.5
  90.3 0.6 constant_dynamic-update-slice_fusion.4
  90.9 0.6 constant_dynamic-update-slice_fusion.3
  91.5 0.6 constant_dynamic-update-slice_fusion.2
  92.1 0.6 constant_dynamic-update-slice_fusion.1
  92.8 0.6 constant_dynamic-update-slice_fusion
  93.4 10.5 %all-to-all-start = ((bf16[32,1,8,3072]{3,2,1,0:T(8,128)(2,1)}), bf16[32,1,8,3072]{3,2,1,0:T(8,128)(2,1)S(1)}, u32[]{:S(2)}, u32[]{:S(2)}) async-start(bf16[32,1,8,3072]{3,2,1,0:T(8,128)(2,1)} %constant_dynamic-update-slice_fusion), calls=%async_computation | async-start | bytes 3145728 | tf_op jit(solution)/shard_map/all_to_all | solution.py:45
  103.9 0.0 all-gather.2.cloned.1.call-done
  104.0 7.7 %fusion.12 = bf16[32,8,1536]{2,1,0:T(8,128)(2,1)} fusion(bf16[256,3072]{1,0:T(8,128)(2,1)} %all-gather.2.cloned.1.call-done, bf16[192,8,24,128]{3,2,1,0:T(8,128)(2,1)} %bitcast.176), kind=kOutput, calls=%fused_computation.11 | convolution fusion | flops 2416312320 | bytes 11796480 | tf_op jit(solution)/shard_map/dot_general | solution.py:59
  111.7 13.7 %all-to-all-done = bf16[32,1,8,3072]{3,2,1,0:T(8,128)(2,1)S(1)} async-done(((bf16[32,1,8,3072]{3,2,1,0:T(8,128)(2,1)}), bf16[32,1,8,3072]{3,2,1,0:T(8,128)(2,1)S(1)}, u32[]{:S(2)}, u32[]{:S(2)}) %all-to-all-start) | async-done | bytes 1572896 | tf_op jit(solution)/shard_map/all_to_all | solution.py:45
  125.4 5.6 %all-to-all-start.1 = ((bf16[32,8,1536]{2,1,0:T(8,128)(2,1)}), bf16[32,8,1536]{2,1,0:T(8,128)(2,1)S(1)}, u32[]{:S(2)}, u32[]{:S(2)}) async-start(bf16[32,8,1536]{2,1,0:T(8,128)(2,1)} %fusion.12), calls=%async_computation.1 | async-start | bytes 1572864 | tf_op jit(solution)/shard_map/all_to_all | solution.py:66
  130.9 2.0 %copy.12 = bf16[1,8,32,3072]{3,2,1,0:T(8,128)(2,1)} copy(bf16[1,8,32,3072]{3,1,0,2:T(8,128)(2,1)S(1)} %bitcast.177) | data formatting | bytes 3145728 | tf_op jit(solution)/shard_map/reshape | solution.py:44
  133.0 2.9 %reshape_reshape.3 = bf16[8,8,12288]{2,1,0:T(8,128)(2,1)S(1)} reshape(bf16[1,8,32,3072]{3,2,1,0:T(8,128)(2,1)} %copy.12) | data formatting | bytes 3145728 | tf_op jit(solution)/shard_map/reshape;reshape | solution.py:53
  135.9 1.0 reduce_sum.21
  136.9 1.5 %collective-permute-start = (bf16[8,12288]{1,0:T(8,128)(2,1)S(1)}, bf16[8,12288]{1,0:T(8,128)(2,1)S(1)}, u32[]{:S(2)}, u32[]{:S(2)}) collective-permute-start(bf16[8,12288]{1,0:T(8,128)(2,1)S(1)} %reduce_sum.21), channel_id=1, source_target_pairs={{0,32},{32,64},{64,96},{96,128},{128,160},{160,192},{192,224},{224... | collective-permute-start | bytes 589832 | tf_op jit(solution)/shard_map/ppermute | solution.py:10
  138.5 4.0 %collective-permute-done = bf16[8,12288]{1,0:T(8,128)(2,1)S(1)} collective-permute-done((bf16[8,12288]{1,0:T(8,128)(2,1)S(1)}, bf16[8,12288]{1,0:T(8,128)(2,1)S(1)}, u32[]{:S(2)}, u32[]{:S(2)}) %collective-permute-start) | collective-permute-done | bytes 196640 | tf_op jit(solution)/shard_map/ppermute | solution.py:10
  142.5 2.1 %all-to-all-done.1 = bf16[32,8,1536]{2,1,0:T(8,128)(2,1)S(1)} async-done(((bf16[32,8,1536]{2,1,0:T(8,128)(2,1)}), bf16[32,8,1536]{2,1,0:T(8,128)(2,1)S(1)}, u32[]{:S(2)}, u32[]{:S(2)}) %all-to-all-start.1) | async-done | bytes 786464 | tf_op jit(solution)/shard_map/all_to_all | solution.py:66
  144.6 0.8 bitcast_reduce_fusion
  145.4 0.7 copy.62
  (3 shorter events, 0.0 us)
Async XLA Ops:
  7.2 58.1 %copy-start = (bf16[256,1536]{1,0:T(8,128)(2,1)S(1)}, bf16[256,1536]{1,0:T(8,128)(2,1)}, u32[]{:S(2)}) copy-start(bf16[256,1536]{1,0:T(8,128)(2,1)} %param.8) | copy-start | bytes 2359300
  7.2 96.8 %all-gather.2.cloned.1.call-start = ((), (), s32[]{:S(2)}) async-start(), calls=%async_computation.2 | async-start | bytes 1769472 | tf_op jit(solution)/shard_map/all_gather | solution.py:60
  93.4 32.0 %all-to-all-start = ((bf16[32,1,8,3072]{3,2,1,0:T(8,128)(2,1)}), bf16[32,1,8,3072]{3,2,1,0:T(8,128)(2,1)S(1)}, u32[]{:S(2)}, u32[]{:S(2)}) async-start(bf16[32,1,8,3072]{3,2,1,0:T(8,128)(2,1)} %constant_dynamic-update-slice_fusion), calls=%async_computation | async-start | bytes 3145728 | tf_op jit(solution)/shard_map/all_to_all | solution.py:45
  125.4 19.2 %all-to-all-start.1 = ((bf16[32,8,1536]{2,1,0:T(8,128)(2,1)}), bf16[32,8,1536]{2,1,0:T(8,128)(2,1)S(1)}, u32[]{:S(2)}, u32[]{:S(2)}) async-start(bf16[32,8,1536]{2,1,0:T(8,128)(2,1)} %fusion.12), calls=%async_computation.1 | async-start | bytes 1572864 | tf_op jit(solution)/shard_map/all_to_all | solution.py:66
  136.9 5.6 %collective-permute-start = (bf16[8,12288]{1,0:T(8,128)(2,1)S(1)}, bf16[8,12288]{1,0:T(8,128)(2,1)S(1)}, u32[]{:S(2)}, u32[]{:S(2)}) collective-permute-start(bf16[8,12288]{1,0:T(8,128)(2,1)S(1)} %reduce_sum.21), channel_id=1, source_target_pairs={{0,32},{32,64},{64,96},{96,128},{128,160},{160,192},{192,224},{224... | collective-permute-start | bytes 589832 | tf_op jit(solution)/shard_map/ppermute | solution.py:10
Sparse Core Ops, SparseCore 0:
  11.0 37.7 all-gather.1
